TPU v7x, 256 devices: a whole 4x4x8 slice. The times are simulated.
256 devices in a mesh: row: 8 (over z_lo, core), col: 32 (over z_hi, y, x).
Axes of the slice: x: 4, y: 4, z: 8 (z_hi: 2, z_lo: 4; z = z_hi * 4 + z_lo), core: 2. Of those that a mesh axis runs over, the one named last changes fastest.
Arguments:
- tokens: bfloat16 [1024, 12288], P('col', 'row'), may hold values from -6 to 6
- up_weight: bfloat16 [12288, 24576], P('row', 'col'), may hold values from -0.109375 to 0.109375
- down_weight: bfloat16 [24576, 12288], P('col', 'row'), may hold values from -0.078125 to 0.078125
- cotangent: bfloat16 [1024, 12288], P('col', 'row'), may hold values from -6 to 6
- up_pattern: int32 [96, 192], P('row', 'col'), may hold values 0 or 1
- down_pattern: int32 [192, 96], P('col', 'row'), may hold values 0 or 1
Outputs:
- input_grad: bfloat16 [1024, 12288], P('col', 'row')
- up_grad: bfloat16 [12288, 24576], P('row', 'col')
- down_grad: bfloat16 [24576, 12288], P('col', 'row')
All inputs are finite; a program needn't handle non-finite values. No bound on the sum of `up_pattern` or of `down_pattern` on one device may be relied on, other than what follows from the above.
Results may differ from a plain program's by a relative error of at most 0.015.
Values may be sent and summed in bfloat16 or wider, within the bound.
A program may use at most 128 MiB of HBM per device.

v0:
```python
import jax
import jax.numpy as jnp
from jax import lax
from jax.sharding import PartitionSpec as P

half_root = 0.7071067811865476
inv_root_tau = 0.3989422804014327


def widen(pattern, height, breadth):
    blocks_down, blocks_across = pattern.shape
    spread = pattern.astype(jnp.bfloat16)[:, None, :, None]
    spread = jnp.broadcast_to(
        spread, (blocks_down, height // blocks_down, blocks_across, breadth // blocks_across)
    )
    return spread.reshape(height, breadth)


def activate(pre, dact):
    cdf = 0.5 * (1.0 + jax.scipy.special.erf(pre * half_root))
    dens = jnp.exp(-0.5 * pre * pre) * inv_root_tau
    active = (pre * cdf).astype(jnp.bfloat16)
    dhid = (dact * (cdf + pre * dens)).astype(jnp.bfloat16)
    return (active, dhid)


def on_device(tokens, up_weight, down_weight, cotangent, up_pattern, down_pattern):
    full_tokens, full_cotangent = (
        lax.all_gather(tokens, "col", axis=0, tiled=True),
        lax.all_gather(cotangent, "col", axis=0, tiled=True),
    )
    up_mask = widen(up_pattern, up_weight.shape[0], up_weight.shape[1])
    down_mask = widen(down_pattern, down_weight.shape[0], down_weight.shape[1])
    up_eff = up_weight * up_mask
    down_eff = down_weight * down_mask
    pre_part = jnp.dot(full_tokens, up_eff, preferred_element_type=jnp.float32)
    dact_part = lax.dot_general(
        full_cotangent, down_eff, (((1,), (1,)), ((), ())), preferred_element_type=jnp.float32
    )
    pre, dact = lax.psum((pre_part, dact_part), "row")
    active, dhid = activate(pre, dact)
    input_grad = lax.psum_scatter(
        lax.dot_general(
            dhid, up_eff, (((1,), (1,)), ((), ())), preferred_element_type=jnp.float32
        ).astype(jnp.bfloat16),
        "col",
        scatter_dimension=0,
        tiled=True,
    )
    factor = 1.0 / jnp.sqrt(jnp.float32(full_tokens.shape[0]))
    up_grad = lax.dot_general(
        full_tokens, dhid, (((0,), (0,)), ((), ())), preferred_element_type=jnp.float32
    )
    up_grad = (up_grad * up_mask.astype(jnp.float32) * factor).astype(jnp.bfloat16)
    down_grad = lax.dot_general(
        active, full_cotangent, (((0,), (0,)), ((), ())), preferred_element_type=jnp.float32
    )
    down_grad = (down_grad * down_mask.astype(jnp.float32) * factor).astype(jnp.bfloat16)
    return (input_grad, up_grad, down_grad)


def solution(mesh):
    return jax.shard_map(
        on_device,
        mesh=mesh,
        in_specs=(
            P("col", "row"),
            P("row", "col"),
            P("col", "row"),
            P("col", "row"),
            P("row", "col"),
            P("col", "row"),
        ),
        out_specs=(P("col", "row"), P("row", "col"), P("col", "row")),
        check_vma=False,
    )
```

profile of v0, /device:TPU:2, one launch (start us, length us, event | category | flops | bytes accessed | tf_op | source)
XLA Modules:
  0.0 640.0 jit_solution(1797469134917920429)
XLA Ops:
  7.2 0.0 all-gather.5.cloned.1.call-start
  7.2 0.7 all-gather.5.cloned.1.call-update
  7.9 0.0 all-gather.3.cloned.1.call-start
  7.9 0.7 all-gather.3.cloned.1.call-update
  8.6 0.0 all-reduce.3.cloned.1.call-start
  8.7 0.7 convert_element_type.28
  9.4 0.1 copy.11
  9.5 0.0 copy-start.2
  9.5 0.9 convert_element_type.27
  10.3 0.5 broadcast_in_dim.5
  10.8 0.4 copy-done.2
  11.2 1.7 fusion.11
  12.9 101.2 %all-gather.5.cloned.1.call-done = bf16[1024,1536]{1,0:T(8,128)(2,1)} async-done(((bf16[32,1536]{1,0:T(8,128)(2,1)}), bf16[1024,1536]{1,0:T(8,128)(2,1)}) %all-gather.5.cloned.1.call-update) | async-done | bytes 3145744 | tf_op jit(solution)/shard_map/all_gather | solution.py:29
  114.1 6.9 %convolution_bitcast_fusion = f32[1024,768]{0,1:T(8,128)} fusion(bf16[1536,768]{1,0:T(8,128)(2,1)} %get-tuple-element.11, bf16[1024,1536]{1,0:T(8,128)(2,1)} %all-gather.5.cloned.1.call-done), kind=kOutput, calls=%fused_computation.18 | convolution fusion | flops 2415919104 | bytes 8650752 | tf_op jit(solution)/shard_map/dot_general | solution.py:36
  121.0 91.3 %all-gather.3.cloned.1.call-done = bf16[1024,1536]{1,0:T(8,128)(2,1)} async-done(((bf16[32,1536]{1,0:T(8,128)(2,1)}), bf16[1024,1536]{1,0:T(8,128)(2,1)}) %all-gather.3.cloned.1.call-update) | async-done | bytes 3145744 | tf_op jit(solution)/shard_map/all_gather | solution.py:30
  212.3 0.0 copy-start.5
  212.3 0.5 broadcast_in_dim.4
  212.7 0.0 copy-start
  212.7 1.7 copy-done
  214.5 0.8 copy-done.5
  215.3 6.0 fusion.9
  221.3 0.0 all-reduce.3.cloned.1.call-update
  221.3 0.2 reduce-scatter.2.cloned.1.call-start
  221.5 143.6 %all-reduce.3.cloned.1.call-done = (f32[1024,768]{0,1:T(8,128)}, f32[1024,768]{0,1:T(8,128)}) async-done(((f32[1024,768]{0,1:T(8,128)}, f32[1024,768]{0,1:T(8,128)}), (f32[1024,768]{0,1:T(8,128)}, f32[1024,768]{0,1:T(8,128)})) %all-reduce.3.cloned.1.call-update) | async-done | bytes 6291472 | tf_op jit(solution)/shard_map/psum | solution.py:40
  365.1 0.0 copy-start.3
  365.1 3.6 fusion.7
  368.8 0.0 copy-start.4
  368.8 1.1 copy-done.4
  369.9 0.0 copy-done.3
  369.9 4.1 convolution_convert_fusion
  374.0 0.0 reduce-scatter.2.cloned.1.call-update
  374.1 2.4 copy.12
  376.5 7.1 %fusion.1 = bf16[1536,768]{0,1:T(8,128)(2,1)} fusion(bf16[1536,768]{0,1:T(8,128)(2,1)} %copy.12, bf16[1024,768]{0,1:T(8,128)(2,1)} %copy-done.4, bf16[1024,1536]{1,0:T(8,128)(2,1)} %all-gather.5.cloned.1.call-done), kind=kOutput, calls=%fused_computation.3 | convolution fusion | flops 2420637696 | bytes 9437184 | tf_op jit(solution)/shard_map/dot_general | solution.py:51
  383.6 0.0 copy-start.1
  383.6 4.4 copy.13
  388.0 0.0 copy-done.1
  388.0 6.9 %multiply_convert_fusion = bf16[768,1536]{1,0:T(8,128)(2,1)} fusion(bf16[1024,1536]{1,0:T(8,128)(2,1)} %all-gather.3.cloned.1.call-done, bf16[96,8,12,128]{3,2,1,0:T(8,128)(2,1)S(1)} %bitcast.33, f32[1024,768]{0,1:T(8,128)} %get-tuple-element.10), kind=kOutput, calls=%fused_computation.4 | convolution fusion | flops 2424569856 | bytes 11010048 | tf_op jit(solution)/shard_map/dot_general | solution.py:55
  394.9 238.5 %reduce-scatter.2.cloned.1.call-done = bf16[32,1536]{1,0:T(8,128)(2,1)} async-done(((bf16[1024,1536]{1,0:T(8,128)(2,1)}), bf16[32,1536]{1,0:T(8,128)(2,1)}) %reduce-scatter.2.cloned.1.call-update) | async-done | bytes 98320 | tf_op jit(solution)/shard_map/reduce_scatter | solution.py:42
Async XLA Ops:
  7.2 106.9 %all-gather.5.cloned.1.call-start = ((), (), s32[]{:S(2)}) async-start(), calls=%async_computation.2 | async-start | bytes 3244032 | tf_op jit(solution)/shard_map/all_gather | solution.py:29
  7.9 204.4 %all-gather.3.cloned.1.call-start = ((), (), s32[]{:S(2)}) async-start(), calls=%async_computation.1 | async-start | bytes 3244032 | tf_op jit(solution)/shard_map/all_gather | solution.py:30
  8.6 356.5 %all-reduce.3.cloned.1.call-start = ((), (), s32[]{:S(2)}) async-start(), calls=%async_computation.4 | async-start | bytes 12582912 | tf_op jit(solution)/shard_map/psum | solution.py:40
  9.5 1.7 copy-start.2
  212.3 3.0 copy-start.5
  212.7 1.7 copy-start
  221.3 412.1 %reduce-scatter.2.cloned.1.call-start = ((), (), s32[]{:S(2)}) async-start(), calls=%async_computation.3 | async-start | bytes 3244032 | tf_op jit(solution)/shard_map/reduce_scatter | solution.py:42
  365.1 4.8 copy-start.3
  368.8 1.1 copy-start.4
  383.6 4.4 copy-start.1
Sparse Core Ops, SparseCore 0:
  11.5 102.5 all-gather.4
  117.5 94.6 all-gather.2
  221.4 143.6 all-reduce.2
  374.2 259.1 reduce-scatter.1
where the time goes:
time: 640 us
  waiting for transfers between devices  576 us (90%)
  matrix products  31.1 us (5%)
  between operations  13.8 us (2%)
  local copies, waits for them, and re-layouts  11.9 us (2%)
  other arithmetic  6.89 us (1%)
    reduce_scatter x1, waiting for transfers between devices, on_device(): lax.psum_scatter(lax.dot_general(dhid, up_eff, (((1,), (1,)), ((), ())),...  238 us
    psum x1, waiting for transfers between devices, on_device(): pre, dact = lax.psum((pre_part, dact_part), 'row')  144 us
    all_gather x1, waiting for transfers between devices, on_device(): lax.all_gather(tokens, 'col', axis=0, tiled=True)  101 us
    all_gather x1, waiting for transfers between devices, on_device(): lax.all_gather(cotangent, 'col', axis=0, tiled=True)  91.3 us
  transfers between devices with their start and end apart: 4, of which 4 were waited for; matrix products, arithmetic and copies ran while one was open for 5% of the time, Pallas kernels for 0%

commit v1 on v0

--- a/solution.py
+++ b/solution.py
@@ -26,7 +26,9 @@
 
 def on_device(tokens, up_weight, down_weight, cotangent, up_pattern, down_pattern):
     full_tokens, full_cotangent = (
-        lax.all_gather(tokens, "col", axis=0, tiled=True),
+        jnp.concatenate(
+            lax.all_to_all(jnp.stack([tokens] * lax.axis_size("col")), "col", 0, 0), axis=0
+        ),
         lax.all_gather(cotangent, "col", axis=0, tiled=True),
     )
     up_mask = widen(up_pattern, up_weight.shape[0], up_weight.shape[1])

time: 640 us -> 589 us (0.920)
  waiting for transfers between devices: 576 us -> 507 us
  starting transfers between devices: 0.34 us -> 14.7 us
    all_gather x1 -> x0, waiting for transfers between devices: 101 us -> none  [on_device(): lax.all_gather(tokens, 'col', axis=0, tiled=True)]
    all_to_all x0 -> x1, waiting for transfers between devices: none -> 69.5 us  [on_device(): lax.all_to_all(jnp.stack([tokens] * lax.axis_size('col')), 'col', 0, 0)]
    all_gather x1, waiting for transfers between devices: 91.3 us -> 55 us  [on_device(): lax.all_gather(cotangent, 'col', axis=0, tiled=True)]
    all_to_all x0 -> x1, starting transfers between devices: none -> 14.4 us  [on_device(): lax.all_to_all(jnp.stack([tokens] * lax.axis_size('col')), 'col', 0, 0)]
where the time goes in v1:
time: 589 us; the launch traced here: 588 us
  waiting for transfers between devices  507 us (86%)
  matrix products  31.1 us (5%)
  starting transfers between devices  14.7 us (2%)
  local copies, waits for them, and re-layouts  14.5 us (2%)
  between operations  13.8 us (2%)
  other arithmetic  7.02 us (1%)
    reduce_scatter x1, waiting for transfers between devices, on_device(): lax.psum_scatter(lax.dot_general(dhid, up_eff, (((1,), (1,)), ((), ())),...  239 us
    psum x1, waiting for transfers between devices, on_device(): pre, dact = lax.psum((pre_part, dact_part), 'row')  144 us
    all_to_all x1, waiting for transfers between devices, on_device(): lax.all_to_all(jnp.stack([tokens] * lax.axis_size('col')), 'col', 0, 0)  69.5 us
    all_gather x1, waiting for transfers between devices, on_device(): lax.all_gather(cotangent, 'col', axis=0, tiled=True)  55 us
    all_to_all x1, starting transfers between devices, on_device(): lax.all_to_all(jnp.stack([tokens] * lax.axis_size('col')), 'col', 0, 0)  14.4 us
  transfers between devices with their start and end apart: 4, of which 4 were waited for; matrix products, arithmetic and copies ran while one was open for 5% of the time, Pallas kernels for 0%

profile of v1, /device:TPU:2, one launch (start us, length us, event | category | flops | bytes accessed | tf_op | source)
XLA Modules:
  0.0 588.5 jit_solution(4444349977251969583)
XLA Ops:
  7.2 3.0 stack.2
  10.1 0.0 copy-start.4
  10.1 0.0 copy-start.5
  10.1 14.4 %all-to-all-start = ((bf16[32,32,1536]{2,1,0:T(8,128)(2,1)}), bf16[32,32,1536]{2,1,0:T(8,128)(2,1)}, u32[]{:S(2)}, u32[]{:S(2)}) async-start(bf16[32,32,1536]{2,1,0:T(8,128)(2,1)} %stack.2), calls=%async_computation | async-start | bytes 6291456 | tf_op jit(solution)/shard_map/all_to_all | solution.py:30
  24.6 0.0 all-gather.2.cloned.1.call-start
  24.6 0.7 all-gather.2.cloned.1.call-update
  25.3 0.0 all-reduce.3.cloned.1.call-start
  25.3 0.0 copy-done.4
  25.4 0.1 copy.11
  25.5 0.0 copy-done.5
  25.5 0.5 broadcast_in_dim.5
  26.0 3.4 fusion.11
  29.3 69.5 %all-to-all-done = bf16[32,32,1536]{2,1,0:T(8,128)(2,1)} async-done(((bf16[32,32,1536]{2,1,0:T(8,128)(2,1)}), bf16[32,32,1536]{2,1,0:T(8,128)(2,1)}, u32[]{:S(2)}, u32[]{:S(2)}) %all-to-all-start) | async-done | bytes 3145760 | tf_op jit(solution)/shard_map/all_to_all | solution.py:30
  98.8 6.9 %convolution_bitcast_fusion = f32[1024,768]{0,1:T(8,128)} fusion(bf16[1536,768]{1,0:T(8,128)(2,1)} %get-tuple-element.11, bf16[1024,1536]{1,0:T(8,128)(2,1)} %bitcast.1), kind=kOutput, calls=%fused_computation.18 | convolution fusion | flops 2415919104 | bytes 8650752 | tf_op jit(solution)/shard_map/dot_general | solution.py:38
  105.7 55.0 %all-gather.2.cloned.1.call-done = bf16[1024,1536]{1,0:T(8,128)(2,1)} async-done(((bf16[32,1536]{1,0:T(8,128)(2,1)}), bf16[1024,1536]{1,0:T(8,128)(2,1)}) %all-gather.2.cloned.1.call-update) | async-done | bytes 3145744 | tf_op jit(solution)/shard_map/all_gather | solution.py:32
  160.7 0.0 copy-start.6
  160.7 0.5 broadcast_in_dim.4
  161.2 0.0 copy-start
  161.2 1.7 copy-done
  162.9 0.8 copy-done.6
  163.7 6.0 %fusion.9 = f32[1024,768]{0,1:T(8,128)} fusion(bf16[1024,1536]{1,0:T(8,128)(2,1)S(1)} %copy-done.6, bf16[768,1536]{1,0:T(8,128)(2,1)} %param.8, bf16[96,8,12,128]{3,2,1,0:T(8,128)(2,1)S(1)} %bitcast.33), kind=kOutput, calls=%fused_computation.17 | convolution fusion | flops 2417098752 | bytes 11010048 | tf_op jit(solution)/shard_map/dot_general | solution.py:39
  169.7 0.0 all-reduce.3.cloned.1.call-update
  169.8 0.2 reduce-scatter.2.cloned.1.call-start
  170.0 143.6 %all-reduce.3.cloned.1.call-done = (f32[1024,768]{0,1:T(8,128)}, f32[1024,768]{0,1:T(8,128)}) async-done(((f32[1024,768]{0,1:T(8,128)}, f32[1024,768]{0,1:T(8,128)}), (f32[1024,768]{0,1:T(8,128)}, f32[1024,768]{0,1:T(8,128)})) %all-reduce.3.cloned.1.call-update) | async-done | bytes 6291472 | tf_op jit(solution)/shard_map/psum | solution.py:42
  313.6 0.0 copy-start.2
  313.6 3.6 fusion.7
  317.2 0.0 copy-start.3
  317.2 1.1 copy-done.3
  318.4 0.0 copy-done.2
  318.4 4.1 convolution_convert_fusion
  322.5 0.0 reduce-scatter.2.cloned.1.call-update
  322.5 2.4 copy.12
  324.9 7.1 %fusion.1 = bf16[1536,768]{0,1:T(8,128)(2,1)} fusion(bf16[1536,768]{0,1:T(8,128)(2,1)} %copy.12, bf16[1024,768]{0,1:T(8,128)(2,1)} %copy-done.3, bf16[1024,1536]{1,0:T(8,128)(2,1)} %bitcast.1), kind=kOutput, calls=%fused_computation.3 | convolution fusion | flops 2420637696 | bytes 9437184 | tf_op jit(solution)/shard_map/dot_general | solution.py:53
  332.0 0.0 copy-start.1
  332.0 4.4 copy.13
  336.5 0.0 copy-done.1
  336.5 6.9 %multiply_convert_fusion = bf16[768,1536]{1,0:T(8,128)(2,1)} fusion(bf16[1024,1536]{1,0:T(8,128)(2,1)} %all-gather.2.cloned.1.call-done, bf16[96,8,12,128]{3,2,1,0:T(8,128)(2,1)S(1)} %bitcast.34, f32[1024,768]{0,1:T(8,128)} %get-tuple-element.10), kind=kOutput, calls=%fused_computation.4 | convolution fusion | flops 2424569856 | bytes 11010048 | tf_op jit(solution)/shard_map/dot_general | solution.py:57
  343.4 238.6 %reduce-scatter.2.cloned.1.call-done = bf16[32,1536]{1,0:T(8,128)(2,1)} async-done(((bf16[1024,1536]{1,0:T(8,128)(2,1)}), bf16[32,1536]{1,0:T(8,128)(2,1)}) %reduce-scatter.2.cloned.1.call-update) | async-done | bytes 98320 | tf_op jit(solution)/shard_map/reduce_scatter | solution.py:44
  (2 shorter events, 0.0 us)
Async XLA Ops:
  10.1 15.2 %copy-start.4 = (s32[12,6]{0,1:T(8,128)S(1)}, s32[12,6]{0,1:T(8,128)}, u32[]{:S(2)}) copy-start(s32[12,6]{0,1:T(8,128)} %param.10) | copy-start | bytes 868
  10.1 15.3 %copy-start.5 = (s32[6,12]{1,0:T(8,128)S(1)}, s32[6,12]{1,0:T(8,128)}, u32[]{:S(2)}) copy-start(s32[6,12]{1,0:T(8,128)} %param.11) | copy-start | bytes 868
  10.1 88.7 %all-to-all-start = ((bf16[32,32,1536]{2,1,0:T(8,128)(2,1)}), bf16[32,32,1536]{2,1,0:T(8,128)(2,1)}, u32[]{:S(2)}, u32[]{:S(2)}) async-start(bf16[32,32,1536]{2,1,0:T(8,128)(2,1)} %stack.2), calls=%async_computation | async-start | bytes 6291456 | tf_op jit(solution)/shard_map/all_to_all | solution.py:30
  24.6 136.1 %all-gather.2.cloned.1.call-start = ((), (), s32[]{:S(2)}) async-start(), calls=%async_computation.2 | async-start | bytes 3244032 | tf_op jit(solution)/shard_map/all_gather | solution.py:32
  25.3 288.3 %all-reduce.3.cloned.1.call-start = ((), (), s32[]{:S(2)}) async-start(), calls=%async_computation.4 | async-start | bytes 12582912 | tf_op jit(solution)/shard_map/psum | solution.py:42
  160.7 3.0 copy-start.6
  161.2 1.7 copy-start
  169.8 412.2 %reduce-scatter.2.cloned.1.call-start = ((), (), s32[]{:S(2)}) async-start(), calls=%async_computation.3 | async-start | bytes 3244032 | tf_op jit(solution)/shard_map/reduce_scatter | solution.py:44
  313.6 4.8 copy-start.2
  317.2 1.1 copy-start.3
  332.0 4.4 copy-start.1
Sparse Core Ops, SparseCore 0:
  28.9 131.7 all-gather.1
  169.9 143.6 all-reduce.2
  322.6 259.2 reduce-scatter.1
